TPU v7x, 256 devices: a whole 4x4x8 slice. The times are simulated.
256 devices in a mesh: cube: 32 (over y, x, core), grid: 8 (over z).
Axes of the slice: x: 4, y: 4, z: 8, core: 2. Of those that a mesh axis runs over, the one named last changes fastest.
Arguments:
- child_update: bfloat16 [8192, 16384], P('cube', 'grid'), may hold values from -6 to 6
- child_panel: bfloat16 [512, 8192], P('grid', 'cube'), may hold values from -6 to 6
- panel_entries: bfloat16 [512, 32768], P('grid', 'cube'), may hold values from -6 to 6
- panel_inverse: bfloat16 [512, 512], replicated, as said below
- block_owner: int32 [1024], replicated, may hold values from 0 to 31, as said below
- child_dest: int32 [512], replicated, may hold values from 0 to 1023, as said below
- child_rows: int32 [512, 16], P('cube'), may hold values from 0 to 15, each once within a row
Outputs:
- schur_update: bfloat16 [32768, 16384], P('cube', 'grid')
- panel_factor: bfloat16 [512, 32768], P('grid', 'cube')
Inputs may be any that keep to these rules, and one draw needn't show every extreme that they name: `block_owner`: row blocks r*128 to (r+1)*128 - 1 form column range r. One cube index owns at most 8 row blocks of one range, and in every draw some cube index owns exactly 8 of some range. Every cube index owns at least one row block. `child_dest`: entry s*16+k names the parent row block into which child row block k of cube index s adds. The 16 child row blocks of one cube index go to blocks of 16 different owners, and in every draw some owner receives a block from every cube index. `panel_inverse`: zero below the diagonal, positive on it.
All inputs are finite; a program needn't handle non-finite values.
Results may differ from a plain program's by a relative error of at most 0.0057.
Values may be sent and summed in bfloat16 or wider, within the bound.
A program may use at most 64 MiB of HBM per device.

v0:
```python
import jax
import jax.numpy as jnp
from jax import lax
from jax.sharding import PartitionSpec as P


def block_ranks(block_owner, range_count, cube_count):
    grouped = block_owner.reshape(range_count, -1)
    owner_ids = jnp.arange(cube_count, dtype=jnp.int32)
    onehot = (grouped[:, :, None] == owner_ids[None, None, :]).astype(jnp.int32)
    running = jnp.cumsum(onehot, axis=1)
    return (jnp.sum(onehot * running, axis=2) - 1).reshape(-1)


def lookup(values_table, wanted):
    matches = wanted[:, None] == jnp.arange(values_table.shape[0], dtype=jnp.int32)[None, :]
    return jnp.sum(jnp.where(matches, values_table[None, :], 0), axis=1)


def local(
    child_update, child_panel, panel_entries, panel_inverse, block_owner, child_dest, child_rows
):
    cube_count = lax.axis_size("cube")
    grid_count = lax.axis_size("grid")
    owner_id = lax.axis_index("cube")
    grid_id = lax.axis_index("grid")
    block_rows = child_rows.shape[1]
    child_slots = child_rows.shape[0]
    col_width = child_update.shape[1]
    panel_part = child_panel.shape[0]
    panel_width = panel_inverse.shape[0]
    block_count = block_owner.shape[0]
    range_blocks = block_count // grid_count
    slot_count = panel_entries.shape[1] // block_rows
    range_slots = slot_count // grid_count
    block_rank = block_ranks(block_owner, grid_count, cube_count)
    range_index = jnp.arange(block_count, dtype=jnp.int32) // range_blocks
    my_slot = jnp.where(block_owner == owner_id, range_index * range_slots + block_rank, -1)
    slot_ids = jnp.arange(slot_count, dtype=jnp.int32)
    live_slot = jnp.sum((my_slot[None, :] == slot_ids[:, None]).astype(jnp.int32), axis=1) > 0
    sent_blocks = lax.dynamic_slice_in_dim(child_dest, owner_id * child_slots, child_slots)
    sent_owner = lookup(block_owner, sent_blocks)
    owner_ids = jnp.arange(cube_count, dtype=jnp.int32)
    routing = (owner_ids[:, None] == sent_owner[None, :]).astype(jnp.bfloat16)
    within = jnp.arange(block_rows, dtype=jnp.int32)
    placing = (child_rows[:, None, :] == within[None, :, None]).astype(jnp.bfloat16)
    update_blocks = child_update.reshape(child_slots, block_rows, col_width)
    placed = jnp.einsum(
        "kij,kjc->kic", placing, update_blocks, preferred_element_type=jnp.float32
    ).astype(jnp.bfloat16)
    send_update = jnp.einsum(
        "ok,kic->oic", routing, placed, preferred_element_type=jnp.float32
    ).astype(jnp.bfloat16)
    panel_blocks = child_panel.reshape(panel_part, child_slots, block_rows)
    placed_panel = jnp.einsum(
        "kij,pkj->pki", placing, panel_blocks, preferred_element_type=jnp.float32
    ).astype(jnp.bfloat16)
    send_panel = jnp.einsum(
        "ok,pki->opi", routing, placed_panel, preferred_element_type=jnp.float32
    ).astype(jnp.bfloat16)
    every_slot = lookup(my_slot, child_dest).reshape(cube_count, child_slots)
    assemble = jnp.sum(
        (every_slot[None, :, :] == slot_ids[:, None, None]).astype(jnp.int32), axis=2
    ).astype(jnp.bfloat16)
    recv_update, recv_panel = (
        lax.all_to_all(send_update, "cube", split_axis=0, concat_axis=0, tiled=True),
        lax.all_to_all(send_panel, "cube", split_axis=0, concat_axis=0, tiled=True),
    )
    gathered = jnp.einsum("js,sic->jic", assemble, recv_update, preferred_element_type=jnp.float32)
    front_update = gathered.reshape(slot_count * block_rows, col_width)
    gathered = jnp.einsum("js,spi->pji", assemble, recv_panel, preferred_element_type=jnp.float32)
    own_rows = panel_entries.reshape(panel_part, slot_count, block_rows)
    own_rows = jnp.where(live_slot[None, :, None], own_rows, jnp.zeros_like(own_rows))
    summed = own_rows.astype(jnp.float32) + gathered
    summed_rows = lax.dot_general(
        lax.all_gather(
            summed.reshape(panel_part, slot_count * block_rows).astype(jnp.bfloat16),
            "grid",
            axis=0,
            tiled=True,
        ),
        panel_inverse,
        (((0,), (0,)), ((), ())),
        preferred_element_type=jnp.float32,
    )
    factor = summed_rows.astype(jnp.bfloat16)
    own_range = lax.dynamic_slice_in_dim(
        factor, grid_id * range_slots * block_rows, range_slots * block_rows, 0
    )
    gathered = lax.all_gather(own_range, "cube", axis=0, tiled=True)
    range_owner = lax.dynamic_slice_in_dim(block_owner, grid_id * range_blocks, range_blocks)
    range_rank = lax.dynamic_slice_in_dim(block_rank, grid_id * range_blocks, range_blocks)
    source = range_owner * range_slots + range_rank
    flat_rows = gathered.reshape(cube_count * range_slots, block_rows * panel_width)
    column_factor = jnp.take(flat_rows, source, axis=0).reshape(
        range_blocks * block_rows, panel_width
    )
    product = lax.dot_general(
        factor, column_factor, (((1,), (1,)), ((), ())), preferred_element_type=jnp.float32
    )
    schur_update = (front_update - product).astype(jnp.bfloat16)
    panel_factor = lax.dynamic_slice_in_dim(factor, grid_id * panel_part, panel_part, 1).T
    return (schur_update, panel_factor)


def solution(mesh):
    placed = (
        P("cube", "grid"),
        P("grid", "cube"),
        P("grid", "cube"),
        P(),
        P(),
        P(),
        P("cube", None),
    )
    return jax.shard_map(
        local,
        mesh=mesh,
        in_specs=placed,
        out_specs=(P("cube", "grid"), P("grid", "cube")),
        check_vma=False,
    )
```

profile of v0, /device:TPU:1, one launch (start us, length us, event | category | flops | bytes accessed | tf_op | source)
XLA Modules:
  0.0 182.5 jit_solution(4184021090647872177)
XLA Ops:
  7.2 0.0 copy-start
  7.2 1.0 copy.68
  8.1 0.8 dynamic_slice.15
  8.9 0.9 select_reduce_fusion.2
  9.8 0.0 copy-start.3
  9.8 0.9 fusion.7
  10.7 0.3 convolution_convert_fusion.3
  11.0 0.1 copy.84
  11.1 0.8 reshape.60
  11.8 8.6 %all-to-all-start.1 = ((bf16[32,2,512]{2,1,0:T(2,128)(2,1)}), bf16[32,2,512]{2,1,0:T(2,128)(2,1)S(1)}, u32[]{:S(2)}, u32[]{:S(2)}) async-start(bf16[32,2,512]{2,1,0:T(2,128)(2,1)} %reshape.60), calls=%async_computation.1 | async-start | bytes 131072 | tf_op jit(solution)/shard_map/all_to_all | solution.py:67
  20.4 0.0 all-gather.3.cloned.1.call-start
  20.5 0.8 copy.60
  21.2 2.5 %select_reduce_fusion.1 = s32[8,128]{0,1:T(8,128)S(1)} fusion(s32[8,128]{0,1:T(8,128)S(1)} %copy.60), kind=kOutput, calls=%fused_computation.20 | output fusion | flops 4324352 | bytes 8192 | tf_op jit(solution)/shard_map/jit(cumsum)/reduce_window_sum | solution.py:11
  23.8 0.7 fusion.24
  24.5 1.1 select_reduce_fusion
  25.6 0.1 convert_reduce_fusion
  25.8 0.1 eq.110
  25.8 1.1 copy.66
  26.9 0.3 copy.67
  27.2 0.2 convert_reduce_fusion.1
  27.4 0.3 all-to-all-done.1
  27.7 0.1 reshape.61
  27.9 0.3 fusion.6
  28.2 0.0 copy-start.2
  28.2 0.3 copy.72
  28.4 0.8 copy.73
  29.2 0.0 all-gather.3.cloned.1.call-update
  29.2 0.0 all-gather.5.cloned.1.call-start
  29.3 35.8 %all-gather.3.cloned.1.call-done = bf16[512,1024]{1,0:T(8,128)(2,1)} async-done(((bf16[64,1024]{1,0:T(8,128)(2,1)}), bf16[512,1024]{1,0:T(8,128)(2,1)}) %all-gather.3.cloned.1.call-update) | async-done | bytes 1048592 | tf_op jit(solution)/shard_map/all_gather | solution.py:76
  65.1 0.0 copy-done.3
  65.1 2.0 %convolution_convert_fusion.2 = bf16[1024,512]{0,1:T(8,128)(2,1)S(1)} fusion(bf16[512,1024]{1,0:T(8,128)(2,1)} %all-gather.3.cloned.1.call-done, bf16[512,512]{1,0:T(8,128)(2,1)S(1)} %copy-done.3), kind=kOutput, calls=%fused_computation.11 | convolution fusion | flops 537395200 | bytes 2621440 | tf_op jit(solution)/shard_map/dot_general | solution.py:75
  67.0 0.0 copy-start.1
  67.1 1.0 copy-done.1
  68.1 0.7 constant_dynamic-slice_fusion
  68.8 0.0 all-gather.5.cloned.1.call-update
  68.8 0.0 copy-done
  68.8 0.0 copy-done.2
  68.8 0.4 convolution_convert_fusion.1
  69.2 1.4 convolution_convert_fusion
  70.7 2.5 %copy.63 = bf16[32,16,2048]{2,1,0:T(8,128)(2,1)} copy(bf16[32,16,2048]{2,0,1:T(8,128)(2,1)S(1)} %convolution_convert_fusion) | data formatting | bytes 4194304 | tf_op jit(solution)/shard_map/convert_element_type | solution.py:53
  73.1 12.6 %all-to-all-start = ((bf16[32,16,2048]{2,1,0:T(8,128)(2,1)}), bf16[32,16,2048]{2,1,0:T(8,128)(2,1)S(1)}, u32[]{:S(2)}, u32[]{:S(2)}) async-start(bf16[32,16,2048]{2,1,0:T(8,128)(2,1)} %copy.63), calls=%async_computation | async-start | bytes 4194304 | tf_op jit(solution)/shard_map/all_to_all | solution.py:66
  85.7 0.8 compare_and_fusion
  86.5 0.1 broadcast_in_dim.74
  86.6 0.1 broadcast_in_dim.75
  86.7 1.6 dynamic-slice_bitcast_fusion
  88.3 25.9 %all-to-all-done = bf16[32,16,2048]{2,1,0:T(8,128)(2,1)S(1)} async-done(((bf16[32,16,2048]{2,1,0:T(8,128)(2,1)}), bf16[32,16,2048]{2,1,0:T(8,128)(2,1)S(1)}, u32[]{:S(2)}, u32[]{:S(2)}) %all-to-all-start) | async-done | bytes 2097184 | tf_op jit(solution)/shard_map/all_to_all | solution.py:66
  114.2 3.3 %fusion.1 = f32[64,16,2048]{2,0,1:T(8,128)S(1)} fusion(bf16[32,16,2048]{2,1,0:T(8,128)(2,1)S(1)} %all-to-all-done, s32[64,32]{0,1:T(8,128)S(1)} %convert_reduce_fusion.1), kind=kOutput, calls=%fused_computation.5 | convolution fusion | flops 134219776 | bytes 10493952 | tf_op jit(solution)/shard_map/js,sic->jic/dot_general | solution.py:69
  117.5 8.1 %copy.65 = f32[64,16,2048]{2,1,0:T(8,128)} copy(f32[64,16,2048]{2,0,1:T(8,128)S(1)} %fusion.1) | data formatting | bytes 16777216 | tf_op jit(solution)/shard_map/js,sic->jic/dot_general | solution.py:69
  125.6 18.3 %all-gather.5.cloned.1.call-done = bf16[4096,512]{0,1:T(8,128)(2,1)} async-done(((bf16[128,512]{0,1:T(8,128)(2,1)}), bf16[4096,512]{0,1:T(8,128)(2,1)}) %all-gather.5.cloned.1.call-update) | async-done | bytes 4194320 | tf_op jit(solution)/shard_map/all_gather | solution.py:90
  143.9 6.4 %copy.74 = bf16[4096,512]{1,0:T(8,128)(2,1)} copy(bf16[4096,512]{0,1:T(8,128)(2,1)} %all-gather.5.cloned.1.call-done) | data formatting | bytes 8388608 | tf_op jit(solution)/shard_map/all_gather | solution.py:90
  150.3 7.4 %reshape.48 = bf16[256,8192]{1,0:T(8,128)(2,1)} reshape(bf16[4096,512]{1,0:T(8,128)(2,1)} %copy.74) | data formatting | bytes 8388608 | tf_op jit(solution)/shard_map/reshape | solution.py:94
  157.7 6.5 %gather_fusion = bf16[128,8192]{1,0:T(8,128)(2,1)S(1)} fusion(bf16[256,8192]{1,0:T(8,128)(2,1)} %reshape.48, s32[1024]{0:T(1024)S(1)} %pad_clamp_fusion), kind=kCustom, calls=%fused_computation | custom fusion | bytes 4194816 | tf_op jit(solution)/shard_map/jit(_take)/gather | solution.py:95
  164.2 2.4 %gather.7 = bf16[2048,512]{1,0:T(8,128)(2,1)} reshape(bf16[128,8192]{1,0:T(8,128)(2,1)S(1)} %gather_fusion) | data formatting | bytes 4194304 | tf_op jit(solution)/shard_map/jit(_take)/gather | solution.py:95
  166.6 9.1 %fusion = bf16[1024,2048]{1,0:T(8,128)(2,1)} fusion(f32[64,16,2048]{2,1,0:T(8,128)} %copy.65, bf16[1024,512]{0,1:T(8,128)(2,1)} %copy-done.1, bf16[2048,512]{1,0:T(8,128)(2,1)} %gather.7, pred[2048]{0:T(1024)(128)(4,1)S(1)} %broadcast_in_dim.75), kind=kOutput, calls=%fused_computation.2 | convolution fusion | flops 2152726528 | bytes 15730688 | tf_op jit(solution)/shard_map/dot_general | solution.py:98
  (4 shorter events, 0.1 us)
Async XLA Ops:
  7.2 61.7 %copy-start = (bf16[256,2048]{1,0:T(8,128)(2,1)S(1)}, bf16[256,2048]{1,0:T(8,128)(2,1)}, u32[]{:S(2)}) copy-start(bf16[256,2048]{1,0:T(8,128)(2,1)} %param.7) | copy-start | bytes 3145732
  9.8 55.3 %copy-start.3 = (bf16[512,512]{1,0:T(8,128)(2,1)S(1)}, bf16[512,512]{1,0:T(8,128)(2,1)}, u32[]{:S(2)}) copy-start(bf16[512,512]{1,0:T(8,128)(2,1)} %param.10) | copy-start | bytes 1572868
  11.8 15.9 %all-to-all-start.1 = ((bf16[32,2,512]{2,1,0:T(2,128)(2,1)}), bf16[32,2,512]{2,1,0:T(2,128)(2,1)S(1)}, u32[]{:S(2)}, u32[]{:S(2)}) async-start(bf16[32,2,512]{2,1,0:T(2,128)(2,1)} %reshape.60), calls=%async_computation.1 | async-start | bytes 131072 | tf_op jit(solution)/shard_map/all_to_all | solution.py:67
  20.4 44.6 %all-gather.3.cloned.1.call-start = ((), (), s32[]{:S(2)}) async-start(), calls=%async_computation.2 | async-start | bytes 1179648 | tf_op jit(solution)/shard_map/all_gather | solution.py:76
  28.2 40.7 %copy-start.2 = (s32[16,16]{1,0:T(8,128)S(1)}, s32[16,16]{1,0:T(8,128)}, u32[]{:S(2)}) copy-start(s32[16,16]{1,0:T(8,128)} %param.13) | copy-start | bytes 3076
  29.2 114.7 %all-gather.5.cloned.1.call-start = ((), (), s32[]{:S(2)}) async-start(), calls=%async_computation.3 | async-start | bytes 4325376 | tf_op jit(solution)/shard_map/all_gather | solution.py:90
  67.0 1.1 copy-start.1
  73.1 41.1 %all-to-all-start = ((bf16[32,16,2048]{2,1,0:T(8,128)(2,1)}), bf16[32,16,2048]{2,1,0:T(8,128)(2,1)S(1)}, u32[]{:S(2)}, u32[]{:S(2)}) async-start(bf16[32,16,2048]{2,1,0:T(8,128)(2,1)} %copy.63), calls=%async_computation | async-start | bytes 4194304 | tf_op jit(solution)/shard_map/all_to_all | solution.py:66
Sparse Core Ops, SparseCore 0:
  29.4 35.6 all-gather.2
  68.9 74.9 all-gather.4
where the time goes:
time: 183 us
  waiting for transfers between devices  80.4 us (44%)
  local copies, waits for them, and re-layouts  42.8 us (23%)
  starting transfers between devices  21.2 us (12%)
  matrix products  17.6 us (10%)
  between operations  14.2 us (8%)
  other arithmetic  6.29 us (3%)
    all_gather x1, waiting for transfers between devices, local(): lax.all_gather(summed.reshape(panel_part, slot_count * block_rows).astype...  35.8 us
    all_to_all x1, waiting for transfers between devices, local(): lax.all_to_all(send_update, 'cube', split_axis=0, concat_axis=0, tiled=True)  25.9 us
    all_gather x1, waiting for transfers between devices, local(): gathered = lax.all_gather(own_range, 'cube', axis=0, tiled=True)  18.3 us
    all_to_all x1, starting transfers between devices, local(): lax.all_to_all(send_update, 'cube', split_axis=0, concat_axis=0, tiled=True)  12.6 us
    dot_general x1, matrix products, local(): lax.dot_general(factor, column_factor, (((1,), (1,)), ((), ())), preferre...  9.06 us
    gather x2, local copies, waits for them, and re-layouts, local(): jnp.take(flat_rows, source, axis=0)  8.91 us
    all_to_all x1, starting transfers between devices, local(): lax.all_to_all(send_panel, 'cube', split_axis=0, concat_axis=0, tiled=True)  8.58 us
    dot_general x1, local copies, waits for them, and re-layouts, local(): jnp.einsum('js,sic->jic', assemble, recv_update, preferred_element_type=j...  8.08 us
  transfers between devices with their start and end apart: 4, of which 4 were waited for; matrix products, arithmetic and copies ran while one was open for 14% of the time, Pallas kernels for 0%

commit v1 on v0

v1 whole, which is shorter than its diff:
```python
import functools

import jax
import jax.numpy as jnp
from jax import lax
from jax.experimental import pallas as pl
from jax.experimental.pallas import tpu as pltpu
from jax.sharding import PartitionSpec as P

MESH = pl.DeviceIdType.MESH
BLOCK = 16
PIECE = 128
EARLY = 16


def iota(shape, dim):
    return lax.broadcasted_iota(jnp.int32, shape, dim)


def onehot(cond, dtype=jnp.bfloat16):
    return jnp.where(cond, 1.0, 0.0).astype(dtype)


def dot(lhs, rhs):
    return jnp.dot(lhs, rhs, preferred_element_type=jnp.float32)


def dot_nt(lhs, rhs):
    return lax.dot_general(lhs, rhs, (((1,), (1,)), ((), ())), preferred_element_type=jnp.float32)


def index_tables(cube, owner_ref, dest_ref, rows_ref):
    owners = owner_ref[...]
    hot = jnp.concatenate(
        [onehot(iota((32, 128), 0) == owners[r : r + 1, :], jnp.float32) for r in range(8)], axis=0
    )
    before = onehot(iota((128, 128), 0) < iota((128, 128), 1))
    running = dot(hot.astype(jnp.bfloat16), before)
    picked = hot * running
    rank = jnp.concatenate(
        [jnp.sum(picked[32 * r : 32 * r + 32], axis=0, keepdims=True) for r in range(8)], axis=0
    )
    owners_f = owners.astype(jnp.float32)
    slot = rank + 8.0 * iota((8, 128), 0).astype(jnp.float32)
    table = jnp.concatenate([owners_f, slot], axis=0).astype(jnp.bfloat16)
    count = jnp.sum(onehot(owners == cube, jnp.float32), axis=1, keepdims=True)
    live = onehot(count > (iota((8, 128), 1) // BLOCK).astype(jnp.float32), jnp.float32)
    source = (owners_f * 8.0 + rank).astype(jnp.int32)
    dest = dest_ref[...]
    child_owner, child_slot = [], []
    for q in range(4):
        row = dest[q : q + 1, :]
        at = onehot(iota((128, 128), 0) == row % 128)
        found = dot(table, at)
        mask = onehot(iota((8, 128), 0) == row // 128, jnp.float32)
        child_owner.append(jnp.sum(found[0:8] * mask, axis=0, keepdims=True))
        child_slot.append(jnp.sum(found[8:16] * mask, axis=0, keepdims=True))
    child_owner = jnp.concatenate(child_owner + child_owner, axis=0)
    child_slot = jnp.concatenate(child_slot + child_slot, axis=0)
    mine = jnp.where(child_owner == cube.astype(jnp.float32), child_slot + 1.0, 0.0)
    group = onehot(iota((128, 128), 0) // BLOCK == iota((128, 128), 1) // BLOCK)
    joined = dot(mine.astype(jnp.bfloat16), group)
    within = (iota((8, 128), 1) % BLOCK).astype(jnp.float32)
    place = jnp.where(joined > 0.5, (joined - 1.0) * BLOCK + within, -1.0).astype(jnp.int32)
    expand = onehot(iota((128, 256), 0) == (cube % 8) * BLOCK + iota((128, 256), 1) // BLOCK)
    own = dot(child_owner.astype(jnp.bfloat16), expand)
    own = jnp.sum(jnp.where(iota((8, 256), 0) == cube // 8, own, 0.0), axis=0, keepdims=True)
    spread = onehot(iota((16, 256), 1) % BLOCK == iota((16, 256), 0))
    rows = dot(rows_ref[...].astype(jnp.float32).astype(jnp.bfloat16), spread)
    rows = jnp.sum(jnp.where(iota((16, 256), 1) // BLOCK == iota((16, 256), 0), rows, 0.0), axis=0, keepdims=True)
    send = (own * BLOCK + rows).astype(jnp.int32)
    return send, place, live, source


def exchange(
    owner_ref,
    dest_ref,
    rows_ref,
    update_ref,
    panel_ref,
    entries_ref,
    inverse_ref,
    recv_update,
    col_factor,
    row_factor,
    place_ref,
    source_ref,
    send_update,
    send_panel,
    recv_panel,
    z_send,
    z_recv,
    piece,
    up_send,
    up_recv,
    pan_send,
    pan_recv,
    za_send,
    za_recv,
    zg_send,
    zg_recv,
    ag_send,
    ag_recv,
    local_sem,
):
    cube = lax.axis_index("cube")
    grid = lax.axis_index("grid")
    core, x, y = cube % 2, (cube // 2) % 4, cube // 8

    def peer(d):
        return ((y + d // 8) % 4 * 4 + (x + d // 2 % 4) % 4) * 2 + (core + d) % 2

    def origin(d):
        return ((y + 4 - d // 8) % 4 * 4 + (x + 4 - d // 2 % 4) % 4) * 2 + (core + d) % 2

    barrier = pltpu.get_barrier_semaphore()

    def greet(d, carry):
        pl.semaphore_signal(barrier, inc=1, device_id={"cube": peer(d)}, device_id_type=MESH)
        return carry

    lax.fori_loop(1, 32, greet, 0)

    def greet_z(d, carry):
        pl.semaphore_signal(barrier, inc=1, device_id={"grid": (grid + d) % 8}, device_id_type=MESH)
        return carry

    lax.fori_loop(1, 8, greet_z, 0)

    send, place, live, source = index_tables(cube, owner_ref, dest_ref, rows_ref)
    place_ref[...] = place
    source_ref[...] = source
    route = onehot(iota((512, 256), 0) == send)
    panel_in = jnp.concatenate([panel_ref[...], jnp.zeros((64, 256), jnp.bfloat16)], axis=0)
    send_panel[...] = dot_nt(route, panel_in).astype(jnp.bfloat16)
    for n in range(4):
        cols = slice(512 * n, 512 * n + 512)
        send_update[:, cols] = dot(route, update_ref[:, cols]).astype(jnp.bfloat16)

    def rows16(owner):
        return pl.ds(pl.multiple_of(owner * BLOCK, BLOCK), BLOCK)

    pl.semaphore_wait(barrier, 38)

    def panel_copy(d):
        to = peer(d)
        return pltpu.make_async_remote_copy(
            send_panel.at[rows16(to), :], recv_panel.at[rows16(cube), :],
            pan_send.at[d], pan_recv.at[d], device_id={"cube": to}, device_id_type=MESH,
        )

    def panel_wait(d):
        return pltpu.make_async_remote_copy(
            send_panel.at[rows16(peer(d)), :], recv_panel.at[rows16(origin(d)), :],
            pan_send.at[d], pan_recv.at[d], device_id={"cube": peer(d)}, device_id_type=MESH,
        )

    def update_copy(d):
        to = peer(d)
        return pltpu.make_async_remote_copy(
            send_update.at[rows16(to), :], recv_update.at[rows16(cube), :],
            up_send.at[d], up_recv.at[d], device_id={"cube": to}, device_id_type=MESH,
        )

    def update_wait(d):
        return pltpu.make_async_remote_copy(
            send_update.at[rows16(peer(d)), :], recv_update.at[rows16(origin(d)), :],
            up_send.at[d], up_recv.at[d], device_id={"cube": peer(d)}, device_id_type=MESH,
        )

    def run(low, high, step):
        def body(d, carry):
            step(d)
            return carry

        lax.fori_loop(low, high, body, 0)

    run(1, 32, lambda d: panel_copy(d).start())
    run(1, EARLY, lambda d: update_copy(d).start())
    own_update = pltpu.make_async_copy(
        send_update.at[rows16(cube), :], recv_update.at[rows16(cube), :], local_sem.at[0]
    )
    own_update.start()
    recv_panel[rows16(cube), :] = send_panel[rows16(cube), :]
    run(1, 32, lambda d: panel_wait(d).wait())

    panel_t = recv_panel[...].astype(jnp.float32).T.astype(jnp.bfloat16)
    for r in range(8):
        gather = jnp.concatenate(
            [onehot(iota((128, 128), 0) + r * 128 == place[q : q + 1, :]) for q in range(4)], axis=1
        )
        total = dot_nt(panel_t, gather)[0:64]
        entries = entries_ref[:, 128 * r : 128 * r + 128].astype(jnp.float32)
        total = total + jnp.where(live[r : r + 1, :] > 0.5, entries, 0.0)
        z_send[r] = total.astype(jnp.bfloat16)

    def zrows(g):
        return pl.ds(pl.multiple_of(g * 64, 64), 64)

    def z_copy(d, into):
        to = (grid + d) % 8
        return pltpu.make_async_remote_copy(
            z_send.at[to], z_recv.at[zrows(into), :],
            za_send.at[d], za_recv.at[d], device_id={"grid": to}, device_id_type=MESH,
        )

    run(1, 8, lambda d: z_copy(d, grid).start())
    z_recv[zrows(grid), :] = z_send[grid]
    run(1, 8, lambda d: z_copy(d, (grid + 8 - d) % 8).wait())
    front = z_recv[...].astype(jnp.float32).T.astype(jnp.bfloat16)
    piece[...] = dot(front, inverse_ref[...]).astype(jnp.bfloat16)

    a = x + core * (y - x)
    b = y + core * (x - y)

    def device(k, p, q):
        return ((q + k * (p - q)) * 4 + p + k * (q - p)) * 2 + k

    def stretch(owner, low, size):
        return pl.ds(pl.multiple_of(owner * PIECE + low, 64), size)

    parts = {"full": (0, 128), "top": (0, 64), "bottom": (64, 64)}

    def ag_copy(m, owner, part, to):
        low, size = parts[part]
        there = col_factor.at[stretch(owner, low, size), :]
        return pltpu.make_async_remote_copy(
            there, there, ag_send.at[m], ag_recv.at[m], device_id={"cube": to}, device_id_type=MESH
        )

    def ag_own(m, to):
        return pltpu.make_async_remote_copy(
            piece, col_factor.at[stretch(cube, 0, 128), :],
            ag_send.at[m], ag_recv.at[m], device_id={"cube": to}, device_id_type=MESH,
        )

    off = (0, 3, 1, 2)
    pa = [(a + o) % 4 for o in off]
    pb = [(b + o) % 4 for o in off]
    a_next, a_prev = device(core, pa[2], b), device(core, pa[1], b)
    b_next, b_prev = device(core, a, pb[2]), device(core, a, pb[1])
    sibling = cube + 1 - 2 * core
    sent = []

    def go(copy):
        copy.start()
        sent.append(copy)

    def got(m, owner, part):
        ag_copy(m, owner, part, a_next).wait_recv()

    def to_sibling(p, q):
        go(ag_copy(20 + 4 * p + q, device(core, pa[p], pb[q]), "full", sibling))

    def phase2(p):
        go(ag_copy(4 + 4 * p, device(core, pa[p], b), "full", b_next))
        go(ag_copy(5 + 4 * p, device(core, pa[p], b), "full", b_prev))
        to_sibling(p, 0)

    def near(p):
        below, above = device(core, pa[p], pb[1]), device(core, pa[p], pb[2])
        got(4 + 4 * p, below, "full")
        go(ag_copy(6 + 4 * p, below, "top", b_next))
        to_sibling(p, 1)
        got(5 + 4 * p, above, "full")
        go(ag_copy(7 + 4 * p, above, "bottom", b_prev))
        to_sibling(p, 2)

    def far(p):
        owner = device(core, pa[p], pb[3])
        got(6 + 4 * p, owner, "top")
        got(7 + 4 * p, owner, "bottom")
        to_sibling(p, 3)

    def z_part(m, owner, part, to):
        low, size = parts[part]
        there = row_factor.at[stretch(owner, low, size), :]
        return pltpu.make_async_remote_copy(
            there, there, zg_send.at[m], zg_recv.at[m], device_id={"grid": to}, device_id_type=MESH
        )

    def z_own(m, to):
        return pltpu.make_async_remote_copy(
            piece, row_factor.at[stretch(grid, 0, 128), :],
            zg_send.at[m], zg_recv.at[m], device_id={"grid": to}, device_id_type=MESH,
        )

    def gz(o):
        return (grid + 8 + o) % 8

    up, down = gz(1), gz(-1)

    def z_hop(k, part_up, part_down):
        z_part(2 * k - 2, gz(-k), "full", up).wait_recv()
        go(z_part(2 * k, gz(-k), part_up, up))
        z_part(2 * k - 1, gz(k), "full", up).wait_recv()
        go(z_part(2 * k + 1, gz(k), part_down, down))

    go(ag_own(0, a_next))
    go(ag_own(1, a_prev))
    go(z_own(0, up))
    go(z_own(1, down))
    go(ag_own(4, b_next))
    go(ag_own(5, b_prev))
    go(ag_own(20, sibling))
    own_col = pltpu.make_async_copy(piece, col_factor.at[stretch(cube, 0, 128), :], local_sem.at[1])
    own_row = pltpu.make_async_copy(piece, row_factor.at[stretch(grid, 0, 128), :], local_sem.at[2])
    own_col.start()
    own_row.start()
    run(EARLY, 32, lambda d: update_copy(d).start())

    left, right, across = device(core, pa[1], b), device(core, pa[2], b), device(core, pa[3], b)
    got(0, left, "full")
    go(ag_copy(2, left, "top", a_next))
    phase2(1)
    got(1, right, "full")
    go(ag_copy(3, right, "bottom", a_prev))
    phase2(2)
    z_hop(1, "full", "full")
    near(0)
    got(2, across, "top")
    got(3, across, "bottom")
    phase2(3)
    z_hop(2, "full", "full")
    near(1)
    far(0)
    near(2)
    z_hop(3, "top", "bottom")
    far(1)
    near(3)
    far(2)
    far(3)
    z_part(6, gz(4), "top", up).wait_recv()
    z_part(7, gz(4), "bottom", up).wait_recv()
    other = 1 - core
    oa = [(b + o) % 4 for o in off]
    ob = [(a + o) % 4 for o in off]
    for p in range(4):
        for q in range(4):
            got(20 + 4 * p + q, device(other, oa[p], ob[q]), "full")
    run(1, 32, lambda d: update_wait(d).wait())
    own_update.wait()
    own_col.wait()
    own_row.wait()
    for copy in sent:
        copy.wait_send()


def combine(source_ref, place_ref, recv_ref, row_ref, col_ref, out_ref, panel_ref, gather, columns):
    step = pl.program_id(0)
    grid = lax.axis_index("grid")
    width = out_ref.shape[1]

    @pl.when(step == 0)
    def _():
        for q in range(4):
            gather[:, 128 * q : 128 * q + 128] = onehot(iota((1024, 128), 0) == place_ref[q : q + 1, :])
        pick = onehot(iota((64, 512), 1) == grid * 64 + iota((64, 512), 0))
        panel_ref[...] = dot_nt(pick, row_ref[...]).astype(jnp.bfloat16)

    for n in range(width // BLOCK):
        source = source_ref[grid, step * (width // BLOCK) + n]
        columns[BLOCK * n : BLOCK * n + BLOCK, :] = col_ref[pl.ds(pl.multiple_of(source * BLOCK, BLOCK), BLOCK), :]
    total = dot(gather[...], recv_ref[...]) - dot_nt(row_ref[...], columns[...])
    out_ref[...] = total.astype(jnp.bfloat16)


def local(child_update, child_panel, panel_entries, panel_inverse, block_owner, child_dest, child_rows):
    vmem = pl.BlockSpec(memory_space=pltpu.VMEM)
    anywhere = pl.BlockSpec(memory_space=pl.ANY)
    bf16 = jnp.bfloat16
    dma = pltpu.SemaphoreType.DMA
    recv_update, col_factor, row_factor, place, source = pl.pallas_call(
        exchange,
        out_shape=(
            jax.ShapeDtypeStruct((512, 2048), bf16),
            jax.ShapeDtypeStruct((4096, 512), bf16),
            jax.ShapeDtypeStruct((1024, 512), bf16),
            jax.ShapeDtypeStruct((8, 128), jnp.int32),
            jax.ShapeDtypeStruct((8, 128), jnp.int32),
        ),
        in_specs=[vmem] * 7,
        out_specs=(anywhere, anywhere, anywhere, vmem, vmem),
        scratch_shapes=[
            pltpu.VMEM((512, 2048), bf16),
            pltpu.VMEM((512, 128), bf16),
            pltpu.VMEM((512, 128), bf16),
            pltpu.VMEM((8, 64, 128), bf16),
            pltpu.VMEM((512, 128), bf16),
            pltpu.VMEM((128, 512), bf16),
            dma((32,)), dma((32,)), dma((32,)), dma((32,)),
            dma((8,)), dma((8,)), dma((8,)), dma((8,)),
            dma((36,)), dma((36,)), dma((3,)),
        ],
        compiler_params=pltpu.CompilerParams(
            collective_id=0, has_side_effects=True, vmem_limit_bytes=24 * 1024 * 1024
        ),
        name="exchange",
    )(
        block_owner.reshape(8, 128), child_dest.reshape(4, 128), child_rows,
        child_update, child_panel, panel_entries, panel_inverse,
    )
    width = 256
    steps = 2048 // width
    out, panel = pl.pallas_call(
        combine,
        out_shape=(jax.ShapeDtypeStruct((1024, 2048), bf16), jax.ShapeDtypeStruct((64, 1024), bf16)),
        grid_spec=pltpu.PrefetchScalarGridSpec(
            num_scalar_prefetch=1,
            grid=(steps,),
            in_specs=[
                pl.BlockSpec((8, 128), lambda i, s: (0, 0)),
                pl.BlockSpec((512, width), lambda i, s: (0, i)),
                pl.BlockSpec((1024, 512), lambda i, s: (0, 0)),
                pl.BlockSpec((4096, 512), lambda i, s: (0, 0)),
            ],
            out_specs=[
                pl.BlockSpec((1024, width), lambda i, s: (0, i)),
                pl.BlockSpec((64, 1024), lambda i, s: (0, 0)),
            ],
            scratch_shapes=[pltpu.VMEM((1024, 512), bf16), pltpu.VMEM((width, 512), bf16)],
        ),
        compiler_params=pltpu.CompilerParams(
            dimension_semantics=("arbitrary",), vmem_limit_bytes=32 * 1024 * 1024
        ),
        name="combine",
    )(source, place, recv_update, row_factor, col_factor)
    return out, panel


def solution(mesh):
    placed = (
        P("cube", "grid"),
        P("grid", "cube"),
        P("grid", "cube"),
        P(),
        P(),
        P(),
        P("cube", None),
    )
    return jax.shard_map(
        local,
        mesh=mesh,
        in_specs=placed,
        out_specs=(P("cube", "grid"), P("grid", "cube")),
        check_vma=False,
    )
```

time: 183 us -> 80.4 us (0.44)
  waiting for transfers between devices: 80.4 us -> 0 us
  Pallas kernels: 0 us -> 72.5 us
  local copies, waits for them, and re-layouts: 42.8 us -> 5.98 us
  starting transfers between devices: 21.2 us -> 0 us
  matrix products: 17.6 us -> 0 us
  between operations: 14.2 us -> 0.65 us
  other arithmetic: 6.29 us -> 0 us
    pallas_call x0 -> x2, Pallas kernels: none -> 72.5 us  [the longest x1 63.9 us: local(): pl.pallas_call(exchange, out_shape=(jax.ShapeDtypeStruct((512, 2048), bf1...]
    all_gather x2 -> x0, waiting for transfers between devices: 54.1 us -> none  [the longest x1 35.8 us: local(): lax.all_gather(summed.reshape(panel_part, slot_count * block_rows).astype...]
    all_to_all x2 -> x0, waiting for transfers between devices: 26.2 us -> none  [the longest x1 25.9 us: local(): lax.all_to_all(send_update, 'cube', split_axis=0, concat_axis=0, tiled=True)]
    all_to_all x2 -> x0, starting transfers between devices: 21.2 us -> none  [the longest x1 12.6 us: local(): lax.all_to_all(send_update, 'cube', split_axis=0, concat_axis=0, tiled=True)]
    dot_general x8 -> x0, matrix products: 17.6 us -> none  [the longest x1 9.06 us: local(): lax.dot_general(factor, column_factor, (((1,), (1,)), ((), ())), preferre...]
    gather x2 -> x0, local copies, waits for them, and re-layouts: 8.91 us -> none  [local(): jnp.take(flat_rows, source, axis=0)]
    dot_general x1 -> x0, local copies, waits for them, and re-layouts: 8.08 us -> none  [local(): jnp.einsum('js,sic->jic', assemble, recv_update, preferred_element_type=j...]
    reshape x2 -> x0, local copies, waits for them, and re-layouts: 7.7 us -> none  [the longest x1 7.41 us: local(): gathered.reshape(cube_count * range_slots, block_rows * panel_width)]
  transfers between devices with their start and end apart: 4 -> 0, of which waited for: 4 -> 0; matrix products, arithmetic and copies ran while one was open for 14% -> 0% of each run, Pallas kernels for 0% -> 0%
where the time goes in v1:
time: 80.4 us; the launch traced here: 79.1 us
  Pallas kernels  72.5 us (90%)
  local copies, waits for them, and re-layouts  5.98 us (7%)
    pallas_call x1, Pallas kernels, local(): pl.pallas_call(exchange, out_shape=(jax.ShapeDtypeStruct((512, 2048), bf1...  63.9 us
    pallas_call x1, Pallas kernels, local(): pl.pallas_call(combine, out_shape=(jax.ShapeDtypeStruct((1024, 2048), bf1...  8.54 us
    unnamed x14, local copies, waits for them, and re-layouts  5.98 us

profile of v1, /device:TPU:1, one launch (start us, length us, event | category | flops | bytes accessed | tf_op | source)
XLA Modules:
  0.0 79.1 jit_solution(2579413457139380150)
XLA Ops:
  0.6 0.0 copy-start
  0.6 1.2 %copy-done = bf16[256,2048]{1,0:T(8,128)(2,1)S(1)} copy-done((bf16[256,2048]{1,0:T(8,128)(2,1)S(1)}, bf16[256,2048]{1,0:T(8,128)(2,1)}, u32[]{:S(2)}) %copy-start) | copy-done | bytes 1048600
  1.9 0.0 copy-start.1
  1.9 1.0 %copy-done.1 = bf16[512,512]{1,0:T(8,128)(2,1)S(1)} copy-done((bf16[512,512]{1,0:T(8,128)(2,1)S(1)}, bf16[512,512]{1,0:T(8,128)(2,1)}, u32[]{:S(2)}) %copy-start.1) | copy-done | bytes 524312
  2.9 0.0 copy-start.2
  2.9 0.9 %copy-done.2 = bf16[64,1024]{1,0:T(8,128)(2,1)S(1)} copy-done((bf16[64,1024]{1,0:T(8,128)(2,1)S(1)}, bf16[64,1024]{1,0:T(8,128)(2,1)}, u32[]{:S(2)}) %copy-start.2) | copy-done | bytes 131096
  3.8 0.0 copy-start.3
  3.8 0.8 copy-done.3
  4.6 0.0 copy-start.4
  4.6 0.7 copy-done.4
  5.3 0.0 copy-start.5
  5.3 0.7 copy-done.5
  5.9 0.0 copy-start.6
  6.0 0.7 copy-done.6
  6.6 63.9 %exchange.1 = (bf16[512,2048]{1,0:T(8,128)(2,1)S(1)}, bf16[4096,512]{1,0:T(8,128)(2,1)S(1)}, bf16[1024,512]{1,0:T(8,128)(2,1)S(1)}, s32[8,128]{1,0:T(8,128)S(1)}, s32[8,128]{1,0:T(8,128)S(1)}) custom-call(s32[8,128]{1,0:T(8,128)S(1)} %bitcast.2, s32[4,128]{1,0:T(4,128)S(1)} %bitcast.3, s32[16,16]{1,0:T(8,128)S(1)} %copy-done.4, ...), custom_call_target="tpu_custom_call" | custom-call | tf_op jit(solution)/shard_map/exchange/pallas_call | solution.py:373
  70.6 8.5 %combine.1 = (bf16[1024,2048]{1,0:T(8,128)(2,1)}, bf16[64,1024]{1,0:T(8,128)(2,1)}) custom-call(s32[8,128]{1,0:T(8,128)S(1)} %get-tuple-element.7.source_ref, s32[8,128]{1,0:T(8,128)S(1)} %get-tuple-element.8.place_ref, bf16[512,2048]{1,0:T(8,128)(2,1)S(1)} %get-tuple-element.9.recv_ref, bf16[1024,512]{1,0:T(8,128)(2,1)S(1)} %get-tuple-element.10.row_ref, ...), custom_call_target="tpu_custom_call" | custom-call | tf_op jit(solution)/shard_map/combine/pallas_call | solution.py:405
Async XLA Ops:
  0.6 1.2 %copy-start = (bf16[256,2048]{1,0:T(8,128)(2,1)S(1)}, bf16[256,2048]{1,0:T(8,128)(2,1)}, u32[]{:S(2)}) copy-start(bf16[256,2048]{1,0:T(8,128)(2,1)} %update_ref.1) | copy-start | bytes 3145732
  1.9 1.0 %copy-start.1 = (bf16[512,512]{1,0:T(8,128)(2,1)S(1)}, bf16[512,512]{1,0:T(8,128)(2,1)}, u32[]{:S(2)}) copy-start(bf16[512,512]{1,0:T(8,128)(2,1)} %inverse_ref.1) | copy-start | bytes 1572868
  2.9 0.9 %copy-start.2 = (bf16[64,1024]{1,0:T(8,128)(2,1)S(1)}, bf16[64,1024]{1,0:T(8,128)(2,1)}, u32[]{:S(2)}) copy-start(bf16[64,1024]{1,0:T(8,128)(2,1)} %entries_ref.1) | copy-start | bytes 393220
  3.8 0.8 copy-start.3
  4.6 0.7 copy-start.4
  5.3 0.7 copy-start.5
  5.9 0.7 copy-start.6

commit v2 on v1

--- a/solution.py
+++ b/solution.py
@@ -10,7 +10,10 @@
 MESH = pl.DeviceIdType.MESH
 BLOCK = 16
 PIECE = 128
-EARLY = 16
+INJECT = (0, 8, 4, 2, 2, 4, 4, 31)
+NEAR_FIRST = False
+DIRECT2 = False
+WIDTH = 512
 
 
 def iota(shape, dim):
@@ -27,6 +30,13 @@
 
 def dot_nt(lhs, rhs):
     return lax.dot_general(lhs, rhs, (((1,), (1,)), ((), ())), preferred_element_type=jnp.float32)
+
+
+def hops(d):
+    return min(d // 8, 4 - d // 8) + min(d // 2 % 4, 4 - d // 2 % 4)
+
+
+ORDER = sorted(range(1, 32), key=hops if NEAR_FIRST else lambda d: -hops(d))
 
 
 def index_tables(cube, owner_ref, dest_ref, rows_ref):
@@ -73,13 +83,13 @@
 
 
 def exchange(
-    owner_ref,
-    dest_ref,
-    rows_ref,
-    update_ref,
-    panel_ref,
-    entries_ref,
-    inverse_ref,
+    owner_hbm,
+    dest_hbm,
+    rows_hbm,
+    panel_hbm,
+    update_hbm,
+    entries_hbm,
+    inverse_hbm,
     recv_update,
     col_factor,
     row_factor,
@@ -102,7 +112,23 @@
     ag_send,
     ag_recv,
     local_sem,
+    load_sem,
+    owner_ref,
+    dest_ref,
+    rows_ref,
+    panel_ref,
+    update_ref,
+    entries_ref,
+    inverse_ref,
 ):
+    sources = (owner_hbm, dest_hbm, rows_hbm, panel_hbm, update_hbm, entries_hbm, inverse_hbm)
+    targets = (owner_ref, dest_ref, rows_ref, panel_ref, update_ref, entries_ref, inverse_ref)
+    loads = [
+        pltpu.make_async_copy(source, target, load_sem.at[n])
+        for n, (source, target) in enumerate(zip(sources, targets))
+    ]
+    for load in loads:
+        load.start()
     cube = lax.axis_index("cube")
     grid = lax.axis_index("grid")
     core, x, y = cube % 2, (cube // 2) % 4, cube // 8
@@ -127,12 +153,16 @@
 
     lax.fori_loop(1, 8, greet_z, 0)
 
+    for load in loads[:3]:
+        load.wait()
     send, place, live, source = index_tables(cube, owner_ref, dest_ref, rows_ref)
     place_ref[...] = place
     source_ref[...] = source
     route = onehot(iota((512, 256), 0) == send)
+    loads[3].wait()
     panel_in = jnp.concatenate([panel_ref[...], jnp.zeros((64, 256), jnp.bfloat16)], axis=0)
     send_panel[...] = dot_nt(route, panel_in).astype(jnp.bfloat16)
+    loads[4].wait()
     for n in range(4):
         cols = slice(512 * n, 512 * n + 512)
         send_update[:, cols] = dot(route, update_ref[:, cols]).astype(jnp.bfloat16)
@@ -176,14 +206,26 @@
         lax.fori_loop(low, high, body, 0)
 
     run(1, 32, lambda d: panel_copy(d).start())
-    run(1, EARLY, lambda d: update_copy(d).start())
+    pending = list(ORDER)
+    stage = iter(INJECT)
+
+    def inject():
+        count = next(stage)
+        for d in pending[:count]:
+            update_copy(d).start()
+        del pending[:count]
+
+    inject()
     own_update = pltpu.make_async_copy(
         send_update.at[rows16(cube), :], recv_update.at[rows16(cube), :], local_sem.at[0]
     )
     own_update.start()
     recv_panel[rows16(cube), :] = send_panel[rows16(cube), :]
     run(1, 32, lambda d: panel_wait(d).wait())
-
+    inject()
+
+    loads[5].wait()
+    loads[6].wait()
     panel_t = recv_panel[...].astype(jnp.float32).T.astype(jnp.bfloat16)
     for r in range(8):
         gather = jnp.concatenate(
@@ -239,6 +281,7 @@
     pb = [(b + o) % 4 for o in off]
     a_next, a_prev = device(core, pa[2], b), device(core, pa[1], b)
     b_next, b_prev = device(core, a, pb[2]), device(core, a, pb[1])
+    b_far = device(core, a, pb[3])
     sibling = cube + 1 - 2 * core
     sent = []
 
@@ -255,21 +298,28 @@
     def phase2(p):
         go(ag_copy(4 + 4 * p, device(core, pa[p], b), "full", b_next))
         go(ag_copy(5 + 4 * p, device(core, pa[p], b), "full", b_prev))
+        if DIRECT2:
+            go(ag_copy(6 + 4 * p, device(core, pa[p], b), "full", b_far))
         to_sibling(p, 0)
 
     def near(p):
         below, above = device(core, pa[p], pb[1]), device(core, pa[p], pb[2])
         got(4 + 4 * p, below, "full")
-        go(ag_copy(6 + 4 * p, below, "top", b_next))
+        if not DIRECT2:
+            go(ag_copy(6 + 4 * p, below, "top", b_next))
         to_sibling(p, 1)
         got(5 + 4 * p, above, "full")
-        go(ag_copy(7 + 4 * p, above, "bottom", b_prev))
+        if not DIRECT2:
+            go(ag_copy(7 + 4 * p, above, "bottom", b_prev))
         to_sibling(p, 2)
 
     def far(p):
         owner = device(core, pa[p], pb[3])
-        got(6 + 4 * p, owner, "top")
-        got(7 + 4 * p, owner, "bottom")
+        if DIRECT2:
+            got(6 + 4 * p, owner, "full")
+        else:
+            got(6 + 4 * p, owner, "top")
+            got(7 + 4 * p, owner, "bottom")
         to_sibling(p, 3)
 
     def z_part(m, owner, part, to):
@@ -298,36 +348,42 @@
 
     go(ag_own(0, a_next))
     go(ag_own(1, a_prev))
+    go(ag_own(2, device(core, pa[3], b)))
     go(z_own(0, up))
     go(z_own(1, down))
     go(ag_own(4, b_next))
     go(ag_own(5, b_prev))
+    if DIRECT2:
+        go(ag_own(6, b_far))
     go(ag_own(20, sibling))
     own_col = pltpu.make_async_copy(piece, col_factor.at[stretch(cube, 0, 128), :], local_sem.at[1])
     own_row = pltpu.make_async_copy(piece, row_factor.at[stretch(grid, 0, 128), :], local_sem.at[2])
     own_col.start()
     own_row.start()
-    run(EARLY, 32, lambda d: update_copy(d).start())
+    inject()
 
     left, right, across = device(core, pa[1], b), device(core, pa[2], b), device(core, pa[3], b)
     got(0, left, "full")
-    go(ag_copy(2, left, "top", a_next))
     phase2(1)
+    inject()
     got(1, right, "full")
-    go(ag_copy(3, right, "bottom", a_prev))
     phase2(2)
+    inject()
+    got(2, across, "full")
+    phase2(3)
+    inject()
     z_hop(1, "full", "full")
     near(0)
-    got(2, across, "top")
-    got(3, across, "bottom")
-    phase2(3)
+    inject()
+    near(1)
     z_hop(2, "full", "full")
-    near(1)
+    near(2)
+    inject()
+    assert not pending
     far(0)
-    near(2)
+    near(3)
     z_hop(3, "top", "bottom")
     far(1)
-    near(3)
     far(2)
     far(3)
     z_part(6, gz(4), "top", up).wait_recv()
@@ -361,7 +417,7 @@
     for n in range(width // BLOCK):
         source = source_ref[grid, step * (width // BLOCK) + n]
         columns[BLOCK * n : BLOCK * n + BLOCK, :] = col_ref[pl.ds(pl.multiple_of(source * BLOCK, BLOCK), BLOCK), :]
-    total = dot(gather[...], recv_ref[...]) - dot_nt(row_ref[...], columns[...])
+    total = dot(gather[...], recv_ref[:, pl.ds(pl.multiple_of(step * width, 128), width)]) - dot_nt(row_ref[...], columns[...])
     out_ref[...] = total.astype(jnp.bfloat16)
 
 
@@ -379,7 +435,7 @@
             jax.ShapeDtypeStruct((8, 128), jnp.int32),
             jax.ShapeDtypeStruct((8, 128), jnp.int32),
         ),
-        in_specs=[vmem] * 7,
+        in_specs=[pl.BlockSpec(memory_space=pltpu.HBM)] * 7,
         out_specs=(anywhere, anywhere, anywhere, vmem, vmem),
         scratch_shapes=[
             pltpu.VMEM((512, 2048), bf16),
@@ -390,17 +446,29 @@
             pltpu.VMEM((128, 512), bf16),
             dma((32,)), dma((32,)), dma((32,)), dma((32,)),
             dma((8,)), dma((8,)), dma((8,)), dma((8,)),
-            dma((36,)), dma((36,)), dma((3,)),
+            dma((36,)), dma((36,)), dma((3,)), dma((7,)),
+            pltpu.VMEM((8, 128), jnp.int32),
+            pltpu.VMEM((4, 128), jnp.int32),
+            pltpu.VMEM((16, 16), jnp.int32),
+            pltpu.VMEM((64, 256), bf16),
+            pltpu.VMEM((256, 2048), bf16),
+            pltpu.VMEM((64, 1024), bf16),
+            pltpu.VMEM((512, 512), bf16),
         ],
         compiler_params=pltpu.CompilerParams(
-            collective_id=0, has_side_effects=True, vmem_limit_bytes=24 * 1024 * 1024
+            collective_id=0, has_side_effects=True, vmem_limit_bytes=26 * 1024 * 1024
         ),
         name="exchange",
     )(
-        block_owner.reshape(8, 128), child_dest.reshape(4, 128), child_rows,
-        child_update, child_panel, panel_entries, panel_inverse,
+        *(
+            pltpu.with_memory_space_constraint(operand, pltpu.HBM)
+            for operand in (
+                block_owner.reshape(8, 128), child_dest.reshape(4, 128), child_rows,
+                child_panel, child_update, panel_entries, panel_inverse,
+            )
+        )
     )
-    width = 256
+    width = WIDTH
     steps = 2048 // width
     out, panel = pl.pallas_call(
         combine,
@@ -408,12 +476,7 @@
         grid_spec=pltpu.PrefetchScalarGridSpec(
             num_scalar_prefetch=1,
             grid=(steps,),
-            in_specs=[
-                pl.BlockSpec((8, 128), lambda i, s: (0, 0)),
-                pl.BlockSpec((512, width), lambda i, s: (0, i)),
-                pl.BlockSpec((1024, 512), lambda i, s: (0, 0)),
-                pl.BlockSpec((4096, 512), lambda i, s: (0, 0)),
-            ],
+            in_specs=[vmem] * 4,
             out_specs=[
                 pl.BlockSpec((1024, width), lambda i, s: (0, i)),
                 pl.BlockSpec((64, 1024), lambda i, s: (0, 0)),

time: 80.4 us -> 66.8 us (0.83); the launches traced: 79.1 us -> 66.7 us
  Pallas kernels: 72.5 us -> 66.1 us
  local copies, waits for them, and re-layouts: 5.98 us -> 0 us
    unnamed x14 -> x0, local copies, waits for them, and re-layouts: 5.98 us -> none
    pallas_call x1, Pallas kernels: 63.9 us -> 58.5 us  [local(): pl.pallas_call(exchange, out_shape=(jax.ShapeDtypeStruct((512, 2048), bf1...]
    pallas_call x1, Pallas kernels: 8.54 us -> 7.57 us  [local(): pl.pallas_call(combine, out_shape=(jax.ShapeDtypeStruct((1024, 2048), bf1...]
where the time goes in v2:
time: 66.8 us; the launch traced here: 66.7 us
  Pallas kernels  66.1 us (99%)
    pallas_call x1, Pallas kernels, local(): pl.pallas_call(exchange, out_shape=(jax.ShapeDtypeStruct((512, 2048), bf1...  58.5 us
    pallas_call x1, Pallas kernels, local(): pl.pallas_call(combine, out_shape=(jax.ShapeDtypeStruct((1024, 2048), bf1...  7.57 us

profile of v2, /device:TPU:1, one launch (start us, length us, event | category | flops | bytes accessed | tf_op | source)
XLA Modules:
  0.0 66.7 jit_solution(8417759202843865996)
XLA Ops:
  0.6 58.5 %exchange.1 = (bf16[512,2048]{1,0:T(8,128)(2,1)S(1)}, bf16[4096,512]{1,0:T(8,128)(2,1)S(1)}, bf16[1024,512]{1,0:T(8,128)(2,1)S(1)}, s32[8,128]{1,0:T(8,128)S(1)}, s32[8,128]{1,0:T(8,128)S(1)}) custom-call(s32[8,128]{1,0:T(8,128)} %bitcast.2, s32[4,128]{1,0:T(4,128)} %bitcast.3, s32[16,16]{1,0:T(8,128)} %rows_hbm.1, bf16[64,256]{1,0:T(8,128)(2,1)} %panel_hbm.1, ...), custom_call_target="tpu_custom_call" | custom-call | tf_op jit(solution)/shard_map/exchange/pallas_call | solution.py:429
  59.1 7.6 %combine.1 = (bf16[1024,2048]{1,0:T(8,128)(2,1)}, bf16[64,1024]{1,0:T(8,128)(2,1)}) custom-call(s32[8,128]{1,0:T(8,128)S(1)} %get-tuple-element.7.source_ref, s32[8,128]{1,0:T(8,128)S(1)} %get-tuple-element.8.place_ref, bf16[512,2048]{1,0:T(8,128)(2,1)S(1)} %get-tuple-element.9.recv_ref, bf16[1024,512]{1,0:T(8,128)(2,1)S(1)} %get-tuple-element.10.row_ref, ...), custom_call_target="tpu_custom_call" | custom-call | tf_op jit(solution)/shard_map/combine/pallas_call | solution.py:473

commit v3 on v2

v3 whole, which is shorter than its diff:
```python
import functools

import jax
import jax.numpy as jnp
from jax import lax
from jax.experimental import pallas as pl
from jax.experimental.pallas import tpu as pltpu
from jax.sharding import PartitionSpec as P

MESH = pl.DeviceIdType.MESH
BLOCK = 16
PIECE = 128
INJECT = (0, 8, 1, 1, 1, 2, 2, 31)
NEAR_FIRST = False
DIRECT2 = (False, False, False, True)
WIDTH = 512
START = 16


def iota(shape, dim):
    return lax.broadcasted_iota(jnp.int32, shape, dim)


def onehot(cond, dtype=jnp.bfloat16):
    return jnp.where(cond, 1.0, 0.0).astype(dtype)


def dot(lhs, rhs):
    return jnp.dot(lhs, rhs, preferred_element_type=jnp.float32)


def dot_nt(lhs, rhs):
    return lax.dot_general(lhs, rhs, (((1,), (1,)), ((), ())), preferred_element_type=jnp.float32)


def hops(d):
    return min(d // 8, 4 - d // 8) + min(d // 2 % 4, 4 - d // 2 % 4)


ORDER = sorted(range(1, 32), key=hops if NEAR_FIRST else lambda d: -hops(d))
SLOT = {d: n + 1 for n, d in enumerate(ORDER)}
SLOT[0] = 0


def send_tables(cube, owner_ref, dest_ref, rows_ref):
    owners = owner_ref[...]
    hot = jnp.concatenate(
        [onehot(iota((32, 128), 0) == owners[r : r + 1, :], jnp.float32) for r in range(8)], axis=0
    )
    before = onehot(iota((128, 128), 0) < iota((128, 128), 1))
    running = dot(hot.astype(jnp.bfloat16), before)
    picked = hot * running
    rank = jnp.concatenate(
        [jnp.sum(picked[32 * r : 32 * r + 32], axis=0, keepdims=True) for r in range(8)], axis=0
    )
    owners_f = owners.astype(jnp.float32)
    slot = rank + 8.0 * iota((8, 128), 0).astype(jnp.float32)
    table = jnp.concatenate([owners_f, slot], axis=0).astype(jnp.bfloat16)
    count = jnp.sum(onehot(owners == cube, jnp.float32), axis=1, keepdims=True)
    live = onehot(count > (iota((8, 128), 1) // BLOCK).astype(jnp.float32), jnp.float32)
    dest = dest_ref[...]
    child_owner, child_slot = [], []
    for q in range(4):
        row = dest[q : q + 1, :]
        at = onehot(iota((128, 128), 0) == row % 128)
        found = dot(table, at)
        mask = onehot(iota((8, 128), 0) == row // 128, jnp.float32)
        child_owner.append(jnp.sum(found[0:8] * mask, axis=0, keepdims=True))
        child_slot.append(jnp.sum(found[8:16] * mask, axis=0, keepdims=True))
    child_owner = jnp.concatenate(child_owner + child_owner, axis=0)
    child_slot = jnp.concatenate(child_slot + child_slot, axis=0)
    expand = onehot(iota((128, 256), 0) == (cube % 8) * BLOCK + iota((128, 256), 1) // BLOCK)
    own = dot(child_owner.astype(jnp.bfloat16), expand)
    own = jnp.sum(jnp.where(iota((8, 256), 0) == cube // 8, own, 0.0), axis=0, keepdims=True)
    spread = onehot(iota((16, 256), 1) % BLOCK == iota((16, 256), 0))
    rows = dot(rows_ref[...].astype(jnp.float32).astype(jnp.bfloat16), spread)
    rows = jnp.sum(jnp.where(iota((16, 256), 1) // BLOCK == iota((16, 256), 0), rows, 0.0), axis=0, keepdims=True)
    send = (own * BLOCK + rows).astype(jnp.int32)
    return send, live, child_owner, child_slot


def receive_table(cube, origins, child_owner, child_slot):
    mine = jnp.where(child_owner == cube.astype(jnp.float32), child_slot + 1.0, 0.0).astype(jnp.bfloat16)
    places = []
    for q in range(4):
        lane = iota((1, 128), 1) // BLOCK
        wanted = jnp.zeros((1, 128), jnp.int32)
        for n in range(8):
            wanted = jnp.where(lane == n, origins[8 * q + n], wanted)
        joined = jnp.zeros((8, 128), jnp.float32)
        for p in range(4):
            pick = onehot(iota((128, 128), 0) // BLOCK + 8 * p == wanted)
            part = dot(mine, pick)
            joined = joined + jnp.where(iota((8, 128), 0) == p, part, 0.0)
        joined = jnp.sum(joined, axis=0, keepdims=True)
        within = (iota((1, 128), 1) % BLOCK).astype(jnp.float32)
        places.append(jnp.where(joined > 0.5, (joined - 1.0) * BLOCK + within, -1.0).astype(jnp.int32))
    return places


def exchange(
    owner_hbm,
    dest_hbm,
    rows_hbm,
    panel_hbm,
    update_hbm,
    entries_hbm,
    inverse_hbm,
    recv_update,
    row_factor,
    gather_ref,
    partial,
    col_factor,
    source_ref,
    source_smem,
    owner_smem,
    columns,
    send_update,
    send_panel,
    recv_panel,
    z_send,
    z_recv,
    piece,
    blocks,
    up_send,
    up_recv,
    pan_send,
    pan_recv,
    za_send,
    za_recv,
    zg_send,
    zg_recv,
    ag_send,
    ag_recv,
    local_sem,
    load_sem,
    owner_ref,
    dest_ref,
    rows_ref,
    panel_ref,
    update_ref,
    entries_ref,
    inverse_ref,
):
    sources = (owner_hbm, dest_hbm, rows_hbm, panel_hbm, update_hbm, entries_hbm, inverse_hbm)
    targets = (owner_ref, dest_ref, rows_ref, panel_ref, update_ref, entries_ref, inverse_ref)
    loads = [
        pltpu.make_async_copy(source, target, load_sem.at[n])
        for n, (source, target) in enumerate(zip(sources, targets))
    ]
    for load in loads:
        load.start()
    to_owners = pltpu.make_async_copy(owner_hbm, owner_smem, local_sem.at[4])
    to_owners.start()
    cube = lax.axis_index("cube")
    grid = lax.axis_index("grid")
    core, x, y = cube % 2, (cube // 2) % 4, cube // 8

    ys = [8 * ((y + k) % 4) for k in range(4)]
    xs = [2 * ((x + k) % 4) for k in range(4)]
    cores = [core, 1 - core]

    def peer(d):
        return ys[d // 8] + xs[d // 2 % 4] + cores[d % 2]

    def origin(d):
        return ys[-(d // 8) % 4] + xs[-(d // 2 % 4) % 4] + cores[d % 2]

    barrier = pltpu.get_barrier_semaphore()

    for d in sorted(range(1, 32), key=hops, reverse=True):
        pl.semaphore_signal(barrier, inc=1, device_id={"cube": peer(d)}, device_id_type=MESH)
    for d in (4, 3, 5, 2, 6, 1, 7):
        pl.semaphore_signal(barrier, inc=1, device_id={"grid": (grid + d) % 8}, device_id_type=MESH)

    for load in loads[:3]:
        load.wait()
    send, live, child_owner, child_slot = send_tables(cube, owner_ref, dest_ref, rows_ref)
    route = onehot(iota((512, 256), 0) == send)
    loads[3].wait()
    panel_in = jnp.concatenate([panel_ref[...], jnp.zeros((64, 256), jnp.bfloat16)], axis=0)
    send_panel[...] = dot_nt(route, panel_in).astype(jnp.bfloat16)

    def rows16(owner):
        return pl.ds(pl.multiple_of(owner * BLOCK, BLOCK), BLOCK)

    def slot16(d):
        return pl.ds(BLOCK * SLOT[d], BLOCK)

    pl.semaphore_wait(barrier, 38)

    def panel_copy(d):
        to = peer(d)
        return pltpu.make_async_remote_copy(
            send_panel.at[rows16(to), :], recv_panel.at[slot16(d), :],
            pan_send.at[d], pan_recv.at[d], device_id={"cube": to}, device_id_type=MESH,
        )

    def panel_wait(d):
        return pltpu.make_async_remote_copy(
            send_panel.at[rows16(peer(d)), :], recv_panel.at[slot16(d), :],
            pan_send.at[d], pan_recv.at[d], device_id={"cube": peer(d)}, device_id_type=MESH,
        )

    def update_copy(d):
        to = peer(d)
        return pltpu.make_async_remote_copy(
            send_update.at[rows16(to), :], recv_update.at[slot16(d), :],
            up_send.at[d], up_recv.at[d], device_id={"cube": to}, device_id_type=MESH,
        )

    def update_wait(d):
        return pltpu.make_async_remote_copy(
            send_update.at[rows16(peer(d)), :], recv_update.at[slot16(d), :],
            up_send.at[d], up_recv.at[d], device_id={"cube": peer(d)}, device_id_type=MESH,
        )

    far_first = sorted(range(1, 32), key=hops, reverse=True)
    for d in far_first:
        panel_copy(d).start()
    loads[4].wait()
    for n in range(4):
        cols = slice(512 * n, 512 * n + 512)
        send_update[:, cols] = dot(route, update_ref[:, cols]).astype(jnp.bfloat16)
    by_slot = {n: d for d, n in SLOT.items()}
    to_owners.wait()
    range_owner = owner_ref[pl.ds(grid, 1), :]
    range_rank = jnp.zeros((1, 128), jnp.int32)
    for n in range(127):
        earlier = (range_owner == owner_smem[grid, n]) & (iota((1, 128), 1) > n)
        range_rank = range_rank + jnp.where(earlier, 1, 0)
    source_ref[...] = range_owner * 8 + range_rank
    places = receive_table(cube, [origin(by_slot[n]) for n in range(32)], child_owner, child_slot)
    pending = list(ORDER)
    stage = iter(INJECT)

    def inject():
        count = next(stage)
        for d in pending[:count]:
            update_copy(d).start()
        del pending[:count]

    inject()
    own_update = pltpu.make_async_copy(
        send_update.at[rows16(cube), :], recv_update.at[slot16(0), :], local_sem.at[0]
    )
    own_update.start()
    recv_panel[slot16(0), :] = send_panel[rows16(cube), :]
    for d in far_first:
        panel_wait(d).wait()
    inject()

    loads[5].wait()
    loads[6].wait()
    panel_t = recv_panel[...].astype(jnp.float32).T.astype(jnp.bfloat16)
    for r in range(8):
        gather = jnp.concatenate(
            [onehot(iota((128, 128), 0) + r * 128 == places[q]) for q in range(4)], axis=1
        )
        gather_ref[128 * r : 128 * r + 128, :] = gather
        total = dot_nt(panel_t, gather)[0:64]
        entries = entries_ref[:, 128 * r : 128 * r + 128].astype(jnp.float32)
        total = total + jnp.where(live[r : r + 1, :] > 0.5, entries, 0.0)
        z_send[r] = total.astype(jnp.bfloat16)

    def zrows(g):
        return pl.ds(pl.multiple_of(g * 64, 64), 64)

    def z_copy(d, into):
        to = (grid + d) % 8
        return pltpu.make_async_remote_copy(
            z_send.at[to], z_recv.at[zrows(into), :],
            za_send.at[d], za_recv.at[d], device_id={"grid": to}, device_id_type=MESH,
        )

    for d in (4, 3, 5, 2, 6, 1, 7):
        z_copy(d, grid).start()
    z_recv[zrows(grid), :] = z_send[grid]
    for d in (4, 3, 5, 2, 6, 1, 7):
        z_copy(d, (grid + 8 - d) % 8).wait()
    front = z_recv[...].astype(jnp.float32).T.astype(jnp.bfloat16)
    own_factor = dot(front, inverse_ref[...]).astype(jnp.bfloat16)
    piece[...] = own_factor
    blocks[...] = own_factor.reshape(8, BLOCK, 512)

    a = x + core * (y - x)
    b = y + core * (x - y)

    def device(k, p, q):
        return ((q + k * (p - q)) * 4 + p + k * (q - p)) * 2 + k

    def stretch(owner, low, size):
        return pl.ds(pl.multiple_of(owner * PIECE + low, 64), size)

    parts = {"full": (0, 128), "top": (0, 64), "bottom": (64, 64)}

    def ag_copy(m, owner, part, to):
        low, size = parts[part]
        there = col_factor.at[pl.ds(owner * 8 + low // BLOCK, size // BLOCK)]
        return pltpu.make_async_remote_copy(
            there, there, ag_send.at[m], ag_recv.at[m], device_id={"cube": to}, device_id_type=MESH
        )

    def ag_own(m, to):
        return pltpu.make_async_remote_copy(
            blocks, col_factor.at[pl.ds(cube * 8, 8)],
            ag_send.at[m], ag_recv.at[m], device_id={"cube": to}, device_id_type=MESH,
        )

    off = (0, 3, 1, 2)
    pa = [(a + o) % 4 for o in off]
    pb = [(b + o) % 4 for o in off]
    a_next, a_prev = device(core, pa[2], b), device(core, pa[1], b)
    b_next, b_prev = device(core, a, pb[2]), device(core, a, pb[1])
    b_far = device(core, a, pb[3])
    sibling = cube + 1 - 2 * core
    sent = []

    def go(copy):
        copy.start()
        sent.append(copy)

    def got(m, owner, part):
        ag_copy(m, owner, part, a_next).wait_recv()

    def to_sibling(p, q):
        go(ag_copy(20 + 4 * p + q, device(core, pa[p], pb[q]), "full", sibling))

    def phase2(p):
        go(ag_copy(4 + 4 * p, device(core, pa[p], b), "full", b_next))
        go(ag_copy(5 + 4 * p, device(core, pa[p], b), "full", b_prev))
        if DIRECT2[p]:
            go(ag_copy(6 + 4 * p, device(core, pa[p], b), "full", b_far))
        to_sibling(p, 0)

    def near(p):
        below, above = device(core, pa[p], pb[1]), device(core, pa[p], pb[2])
        got(4 + 4 * p, below, "full")
        if not DIRECT2[p]:
            go(ag_copy(6 + 4 * p, below, "top", b_next))
        to_sibling(p, 1)
        got(5 + 4 * p, above, "full")
        if not DIRECT2[p]:
            go(ag_copy(7 + 4 * p, above, "bottom", b_prev))
        to_sibling(p, 2)

    def far(p):
        owner = device(core, pa[p], pb[3])
        if DIRECT2[p]:
            got(6 + 4 * p, owner, "full")
        else:
            got(6 + 4 * p, owner, "top")
            got(7 + 4 * p, owner, "bottom")
        to_sibling(p, 3)

    def z_part(m, owner, part, to):
        low, size = parts[part]
        there = row_factor.at[stretch(owner, low, size), :]
        return pltpu.make_async_remote_copy(
            there, there, zg_send.at[m], zg_recv.at[m], device_id={"grid": to}, device_id_type=MESH
        )

    def z_own(m, to):
        return pltpu.make_async_remote_copy(
            piece, row_factor.at[stretch(grid, 0, 128), :],
            zg_send.at[m], zg_recv.at[m], device_id={"grid": to}, device_id_type=MESH,
        )

    def gz(o):
        return (grid + 8 + o) % 8

    def z_got(m, owner, part):
        z_part(m, owner, part, gz(1)).wait_recv()

    def z_relay():
        z_got(2, gz(-2), "full")
        go(z_part(4, gz(-2), "full", gz(1)))
        go(z_part(6, gz(-2), "top", gz(2)))
        z_got(3, gz(2), "full")
        go(z_part(5, gz(2), "full", gz(-1)))
        go(z_part(7, gz(2), "bottom", gz(-2)))

    go(ag_own(0, a_next))
    go(ag_own(1, a_prev))
    go(ag_own(2, device(core, pa[3], b)))
    go(z_own(2, gz(2)))
    go(z_own(3, gz(-2)))
    go(z_own(0, gz(1)))
    go(z_own(1, gz(-1)))
    go(ag_own(4, b_next))
    go(ag_own(5, b_prev))
    if DIRECT2[0]:
        go(ag_own(6, b_far))
    go(ag_own(20, sibling))
    own_col = pltpu.make_async_copy(blocks, col_factor.at[pl.ds(cube * 8, 8)], local_sem.at[1])
    own_row = pltpu.make_async_copy(piece, row_factor.at[stretch(grid, 0, 128), :], local_sem.at[2])
    own_col.start()
    to_smem = pltpu.make_async_copy(source_ref, source_smem, local_sem.at[3])
    to_smem.start()
    own_row.start()
    inject()

    left, right, across = device(core, pa[1], b), device(core, pa[2], b), device(core, pa[3], b)
    got(0, left, "full")
    phase2(1)
    inject()
    got(1, right, "full")
    phase2(2)
    inject()
    near(0)
    got(2, across, "full")
    phase2(3)
    inject()
    z_relay()
    near(1)
    inject()
    near(2)
    far(0)
    near(3)
    inject()
    assert not pending
    far(1)
    far(2)
    far(3)
    for d in ORDER[: START - 1]:
        update_wait(d).wait()
    own_update.wait()
    head = BLOCK * START
    for n in range(8):
        cols = slice(256 * n, 256 * n + 256)
        partial[:, cols] = dot(gather_ref[:, 0:head], recv_update[0:head, cols])
    z_got(0, gz(-1), "full")
    z_got(1, gz(1), "full")
    z_got(4, gz(-3), "full")
    z_got(5, gz(3), "full")
    z_got(6, gz(4), "top")
    z_got(7, gz(4), "bottom")
    other = 1 - core
    oa = [(b + o) % 4 for o in off]
    ob = [(a + o) % 4 for o in off]
    for p in range(4):
        for q in range(4):
            got(20 + 4 * p + q, device(other, oa[p], ob[q]), "full")
    own_col.wait()
    own_row.wait()
    to_smem.wait()
    for n in range(128):
        row = source_smem[0, n]
        columns[BLOCK * n : BLOCK * n + BLOCK, :] = col_factor[row]
    for n in range(8):
        cols = slice(256 * n, 256 * n + 256)
        partial[:, cols] = partial[:, cols] - dot_nt(row_factor[...], columns[cols, :])
    for d in ORDER[START - 1 :]:
        update_wait(d).wait()
    for copy in sent:
        copy.wait_send()


def combine(recv_ref, row_ref, gather_ref, partial_ref, out_ref, panel_ref):
    step = pl.program_id(0)
    grid = lax.axis_index("grid")
    width = out_ref.shape[1]
    head = BLOCK * START

    @pl.when(step == 0)
    def _():
        pick = onehot(iota((64, 512), 1) == grid * 64 + iota((64, 512), 0))
        panel_ref[...] = dot_nt(pick, row_ref[...]).astype(jnp.bfloat16)

    cols = pl.ds(pl.multiple_of(step * width, 128), width)
    total = partial_ref[:, cols] + dot(gather_ref[:, head:512], recv_ref[head:512, cols])
    out_ref[...] = total.astype(jnp.bfloat16)


def local(child_update, child_panel, panel_entries, panel_inverse, block_owner, child_dest, child_rows):
    vmem = pl.BlockSpec(memory_space=pltpu.VMEM)
    bf16 = jnp.bfloat16
    dma = pltpu.SemaphoreType.DMA
    recv_update, row_factor, gather, partial = pl.pallas_call(
        exchange,
        out_shape=(
            jax.ShapeDtypeStruct((512, 2048), bf16),
            jax.ShapeDtypeStruct((1024, 512), bf16),
            jax.ShapeDtypeStruct((1024, 512), bf16),
            jax.ShapeDtypeStruct((1024, 2048), jnp.float32),
        ),
        in_specs=[pl.BlockSpec(memory_space=pltpu.HBM)] * 7,
        out_specs=(vmem, vmem, vmem, vmem),
        scratch_shapes=[
            pltpu.VMEM((256, BLOCK, 512), bf16),
            pltpu.VMEM((1, 128), jnp.int32),
            pltpu.SMEM((1, 128), jnp.int32),
            pltpu.SMEM((8, 128), jnp.int32),
            pltpu.VMEM((2048, 512), bf16),
            pltpu.VMEM((512, 2048), bf16),
            pltpu.VMEM((512, 128), bf16),
            pltpu.VMEM((512, 128), bf16),
            pltpu.VMEM((8, 64, 128), bf16),
            pltpu.VMEM((512, 128), bf16),
            pltpu.VMEM((128, 512), bf16),
            pltpu.VMEM((8, BLOCK, 512), bf16),
            dma((32,)), dma((32,)), dma((32,)), dma((32,)),
            dma((8,)), dma((8,)), dma((8,)), dma((8,)),
            dma((36,)), dma((36,)), dma((5,)), dma((7,)),
            pltpu.VMEM((8, 128), jnp.int32),
            pltpu.VMEM((4, 128), jnp.int32),
            pltpu.VMEM((16, 16), jnp.int32),
            pltpu.VMEM((64, 256), bf16),
            pltpu.VMEM((256, 2048), bf16),
            pltpu.VMEM((64, 1024), bf16),
            pltpu.VMEM((512, 512), bf16),
        ],
        compiler_params=pltpu.CompilerParams(
            collective_id=0, has_side_effects=True, vmem_limit_bytes=30 * 1024 * 1024
        ),
        name="exchange",
    )(
        *(
            pltpu.with_memory_space_constraint(operand, pltpu.HBM)
            for operand in (
                block_owner.reshape(8, 128), child_dest.reshape(4, 128), child_rows,
                child_panel, child_update, panel_entries, panel_inverse,
            )
        )
    )
    width = WIDTH
    steps = 2048 // width
    out, panel = pl.pallas_call(
        combine,
        out_shape=(jax.ShapeDtypeStruct((1024, 2048), bf16), jax.ShapeDtypeStruct((64, 1024), bf16)),
        grid=(steps,),
        in_specs=[vmem] * 4,
        out_specs=(
            pl.BlockSpec((1024, width), lambda i: (0, i)),
            pl.BlockSpec((64, 1024), lambda i: (0, 0)),
        ),
        compiler_params=pltpu.CompilerParams(
            dimension_semantics=("arbitrary",), vmem_limit_bytes=32 * 1024 * 1024
        ),
        name="combine",
    )(recv_update, row_factor, gather, partial)
    return out, panel


def solution(mesh):
    placed = (
        P("cube", "grid"),
        P("grid", "cube"),
        P("grid", "cube"),
        P(),
        P(),
        P(),
        P("cube", None),
    )
    return jax.shard_map(
        local,
        mesh=mesh,
        in_specs=placed,
        out_specs=(P("cube", "grid"), P("grid", "cube")),
        check_vma=False,
    )
```

time: 66.8 us -> 62.9 us (0.942)
  Pallas kernels: 66.1 us -> 62.1 us
    pallas_call x1, Pallas kernels: 7.57 us -> 3.74 us  [local(): pl.pallas_call(combine, out_shape=(jax.ShapeDtypeStruct((1024, 2048), bf1...]
where the time goes in v3:
time: 62.9 us; the launch traced here: 62.8 us
  Pallas kernels  62.1 us (99%)
  between operations  0.64 us (1%)
    pallas_call x1, Pallas kernels, local(): pl.pallas_call(exchange, out_shape=(jax.ShapeDtypeStruct((512, 2048), bf1...  58.4 us
    pallas_call x1, Pallas kernels, local(): pl.pallas_call(combine, out_shape=(jax.ShapeDtypeStruct((1024, 2048), bf1...  3.74 us

profile of v3, /device:TPU:1, one launch (start us, length us, event | category | flops | bytes accessed | tf_op | source)
XLA Modules:
  0.0 62.8 jit_solution(12907712855358901519)
XLA Ops:
  0.6 58.4 %exchange.1 = (bf16[512,2048]{1,0:T(8,128)(2,1)S(1)}, bf16[1024,512]{1,0:T(8,128)(2,1)S(1)}, bf16[1024,512]{1,0:T(8,128)(2,1)S(1)}, f32[1024,2048]{1,0:T(8,128)S(1)}) custom-call(s32[8,128]{1,0:T(8,128)} %bitcast.2, s32[4,128]{1,0:T(4,128)} %bitcast.3, s32[16,16]{1,0:T(8,128)} %rows_hbm.1, bf16[64,256]{1,0:T(8,128)(2,1)} %panel_hbm.1, ...), custom_call_target="tpu_custom_call" | custom-call | tf_op jit(solution)/shard_map/exchange/pallas_call | solution.py:479
  59.0 3.7 %combine.1 = (bf16[1024,2048]{1,0:T(8,128)(2,1)}, bf16[64,1024]{1,0:T(8,128)(2,1)}) custom-call(bf16[512,2048]{1,0:T(8,128)(2,1)S(1)} %get-tuple-element.6.recv_ref, bf16[1024,512]{1,0:T(8,128)(2,1)S(1)} %get-tuple-element.7.row_ref, bf16[1024,512]{1,0:T(8,128)(2,1)S(1)} %get-tuple-element.8.gather_ref, f32[1024,2048]{1,0:T(8,128)S(1)} %get-tuple-element.9.partial_ref), custom_call_target="tpu_custom_call" | custom-call | tf_op jit(solution)/shard_map/combine/pallas_call | solution.py:528

commit v4 on v3

--- a/solution.py
+++ b/solution.py
@@ -10,7 +10,7 @@
 MESH = pl.DeviceIdType.MESH
 BLOCK = 16
 PIECE = 128
-INJECT = (0, 8, 1, 1, 1, 2, 2, 31)
+INJECT = (0, 8, 1, 1, 1, 1, 1, 31)
 NEAR_FIRST = False
 DIRECT2 = (False, False, False, True)
 WIDTH = 512
@@ -223,13 +223,6 @@
         cols = slice(512 * n, 512 * n + 512)
         send_update[:, cols] = dot(route, update_ref[:, cols]).astype(jnp.bfloat16)
     by_slot = {n: d for d, n in SLOT.items()}
-    to_owners.wait()
-    range_owner = owner_ref[pl.ds(grid, 1), :]
-    range_rank = jnp.zeros((1, 128), jnp.int32)
-    for n in range(127):
-        earlier = (range_owner == owner_smem[grid, n]) & (iota((1, 128), 1) > n)
-        range_rank = range_rank + jnp.where(earlier, 1, 0)
-    source_ref[...] = range_owner * 8 + range_rank
     places = receive_table(cube, [origin(by_slot[n]) for n in range(32)], child_owner, child_slot)
     pending = list(ORDER)
     stage = iter(INJECT)
@@ -246,6 +239,11 @@
     )
     own_update.start()
     recv_panel[slot16(0), :] = send_panel[rows16(cube), :]
+    for r in range(8):
+        gather = jnp.concatenate(
+            [onehot(iota((128, 128), 0) + r * 128 == places[q]) for q in range(4)], axis=1
+        )
+        gather_ref[128 * r : 128 * r + 128, :] = gather
     for d in far_first:
         panel_wait(d).wait()
     inject()
@@ -254,11 +252,7 @@
     loads[6].wait()
     panel_t = recv_panel[...].astype(jnp.float32).T.astype(jnp.bfloat16)
     for r in range(8):
-        gather = jnp.concatenate(
-            [onehot(iota((128, 128), 0) + r * 128 == places[q]) for q in range(4)], axis=1
-        )
-        gather_ref[128 * r : 128 * r + 128, :] = gather
-        total = dot_nt(panel_t, gather)[0:64]
+        total = dot_nt(panel_t, gather_ref[128 * r : 128 * r + 128, :])[0:64]
         entries = entries_ref[:, 128 * r : 128 * r + 128].astype(jnp.float32)
         total = total + jnp.where(live[r : r + 1, :] > 0.5, entries, 0.0)
         z_send[r] = total.astype(jnp.bfloat16)
@@ -395,12 +389,17 @@
     own_col = pltpu.make_async_copy(blocks, col_factor.at[pl.ds(cube * 8, 8)], local_sem.at[1])
     own_row = pltpu.make_async_copy(piece, row_factor.at[stretch(grid, 0, 128), :], local_sem.at[2])
     own_col.start()
-    to_smem = pltpu.make_async_copy(source_ref, source_smem, local_sem.at[3])
-    to_smem.start()
     own_row.start()
     inject()
 
     left, right, across = device(core, pa[1], b), device(core, pa[2], b), device(core, pa[3], b)
+    to_owners.wait()
+    range_owner = owner_ref[pl.ds(grid, 1), :]
+    range_rank = jnp.zeros((1, 128), jnp.int32)
+    for n in range(127):
+        earlier = (range_owner == owner_smem[grid, n]) & (iota((1, 128), 1) > n)
+        range_rank = range_rank + jnp.where(earlier, 1, 0)
+    source_ref[...] = range_owner * 8 + range_rank
     got(0, left, "full")
     phase2(1)
     inject()
@@ -411,6 +410,8 @@
     got(2, across, "full")
     phase2(3)
     inject()
+    to_smem = pltpu.make_async_copy(source_ref, source_smem, local_sem.at[3])
+    to_smem.start()
     z_relay()
     near(1)
     inject()

time: 62.9 us -> 61.8 us (0.983)
  Pallas kernels: 62.1 us -> 61 us
    pallas_call x1, Pallas kernels: 58.4 us -> 57.3 us  [local(): pl.pallas_call(exchange, out_shape=(jax.ShapeDtypeStruct((512, 2048), bf1...]
where the time goes in v4:
time: 61.8 us; the launch traced here: 61.7 us
  Pallas kernels  61 us (99%)
  between operations  0.64 us (1%)
    pallas_call x1, Pallas kernels, local(): pl.pallas_call(exchange, out_shape=(jax.ShapeDtypeStruct((512, 2048), bf1...  57.3 us
    pallas_call x1, Pallas kernels, local(): pl.pallas_call(combine, out_shape=(jax.ShapeDtypeStruct((1024, 2048), bf1...  3.74 us

profile of v4, /device:TPU:1, one launch (start us, length us, event | category | flops | bytes accessed | tf_op | source)
XLA Modules:
  0.0 61.7 jit_solution(5412883501852088131)
XLA Ops:
  0.6 57.3 %exchange.1 = (bf16[512,2048]{1,0:T(8,128)(2,1)S(1)}, bf16[1024,512]{1,0:T(8,128)(2,1)S(1)}, bf16[1024,512]{1,0:T(8,128)(2,1)S(1)}, f32[1024,2048]{1,0:T(8,128)S(1)}) custom-call(s32[8,128]{1,0:T(8,128)} %bitcast.2, s32[4,128]{1,0:T(4,128)} %bitcast.3, s32[16,16]{1,0:T(8,128)} %rows_hbm.1, bf16[64,256]{1,0:T(8,128)(2,1)} %panel_hbm.1, ...), custom_call_target="tpu_custom_call" | custom-call | tf_op jit(solution)/shard_map/exchange/pallas_call | solution.py:480
  57.9 3.7 %combine.1 = (bf16[1024,2048]{1,0:T(8,128)(2,1)}, bf16[64,1024]{1,0:T(8,128)(2,1)}) custom-call(bf16[512,2048]{1,0:T(8,128)(2,1)S(1)} %get-tuple-element.6.recv_ref, bf16[1024,512]{1,0:T(8,128)(2,1)S(1)} %get-tuple-element.7.row_ref, bf16[1024,512]{1,0:T(8,128)(2,1)S(1)} %get-tuple-element.8.gather_ref, f32[1024,2048]{1,0:T(8,128)S(1)} %get-tuple-element.9.partial_ref), custom_call_target="tpu_custom_call" | custom-call | tf_op jit(solution)/shard_map/combine/pallas_call | solution.py:529
